TPU v7x, 256 devices: a whole 4x4x8 slice. The times are simulated.
256 devices in a mesh: area: 16 (over x, y), sec: 16 (over z, core).
Axes of the slice: x: 4, y: 4, z: 8, core: 2. Of those that a mesh axis runs over, the one named last changes fastest.
Arguments:
- spikes: int32 [16, 3, 16384], P('area', None, 'sec'), may hold values 0 or 1
- intra_weight: float32 [16, 128, 8, 128, 128], P('area', 'sec'), may hold values from -0.5 to 0.5
- intra_dest: int32 [16, 128, 8], P('area'), may hold values from 0 to 127, all different within a row
- inter_weight: float32 [16, 128, 2, 128, 128], P('area', 'sec'), may hold values from -0.5 to 0.5
- inter_target: int32 [16, 16, 2], P(None, 'sec'), may hold values from 0 to 15, all different within a row
- v_init: float32 [16, 16384], P('area', 'sec'), may hold values from 0 to 1
- leak: float32 [16, 16384], P('area', 'sec'), may hold values from 0.3 to 0.95
Outputs:
- potential: float32 [16, 16384], P('area', 'sec')
Inputs may be any that keep to these rules, and one draw needn't show every extreme that they name: `intra_dest`: the 8 target blocks of a source block are distinct; some blocks receive far more synapse blocks than others. `inter_target`: the 2 target areas of a section are distinct; some areas are targeted far more often than others.
All inputs are finite; a program needn't handle non-finite values. No bound on the sum of `spikes` on one device may be relied on, other than what follows from the above.
Results may differ from a plain program's by a relative error of at most 0.000058.
Values sent between devices are 32-bit elements; how exact they have to be, the bound alone decides.
A program may use at most 64 MiB of HBM per device.

v0:
```python
import jax
import jax.numpy as jnp
from jax import lax
from jax.sharding import PartitionSpec as P


def body(spikes, intra_weight, intra_dest, inter_weight, inter_target, v_init, leak):
    blocks = intra_weight.shape[1]
    width = intra_weight.shape[-1]
    steps = spikes.shape[1]
    columns = steps * width
    later = (steps - 1) * width
    section = lax.axis_index("sec")
    area_here = lax.axis_index("area")
    block_count = intra_dest.shape[1]
    spiking = spikes[0].astype(jnp.float32).reshape(steps, blocks, width)
    previous = spiking[:-1]
    intra_part = jnp.einsum(
        "tkn,kfnm->kftm", spiking, intra_weight[0], precision=lax.Precision.HIGHEST
    )
    fanout = intra_part.shape[1]
    intra_rows = intra_part.reshape(blocks * fanout, columns)
    dest_flat = intra_dest[0].reshape(-1)
    my_dest = lax.dynamic_slice_in_dim(dest_flat, section * blocks * fanout, blocks * fanout, 0)
    picker = (jnp.arange(block_count, dtype=jnp.int32)[:, None] == my_dest[None, :]).astype(
        jnp.float32
    )
    block_grid = jnp.dot(
        picker, intra_rows, precision=lax.Precision.HIGHEST, preferred_element_type=jnp.float32
    )
    intra_current = lax.psum_scatter(block_grid, "sec", scatter_dimension=0, tiled=True)
    inter_part = jnp.einsum(
        "tkn,kjnm->kjtm", previous, inter_weight[0], precision=lax.Precision.HIGHEST
    )
    targets_all = inter_target[:, 0, :]
    fan_areas = targets_all.shape[1]
    picker = (targets_all == area_here).astype(jnp.float32)
    inter_current = jnp.einsum(
        "aj,akjx->kx",
        picker,
        lax.all_gather(inter_part.reshape(1, blocks, fan_areas, later), "area", axis=0, tiled=True),
        precision=lax.Precision.HIGHEST,
    )
    inter_full = jnp.concatenate([jnp.zeros((blocks, width), jnp.float32), inter_current], axis=1)
    current = (intra_current + inter_full).reshape(blocks, steps, width)
    current = current.transpose(1, 0, 2).reshape(steps, blocks * width)
    drive = spikes[0].astype(jnp.float32)
    potential = v_init[0]
    decay = leak[0]
    for moment in range(steps):
        potential = decay * potential * (1.0 - drive[moment]) + current[moment]
    return potential[None]


def solution(mesh):
    in_specs = (
        P("area", None, "sec"),
        P("area", "sec", None, None, None),
        P("area", None, None),
        P("area", "sec", None, None, None),
        P(None, "sec", None),
        P("area", "sec"),
        P("area", "sec"),
    )
    out_specs = P("area", "sec")
    return jax.shard_map(body, mesh=mesh, in_specs=in_specs, out_specs=out_specs, check_vma=False)
```

profile of v0, /device:TPU:1, one launch (start us, length us, event | category | flops | bytes accessed | tf_op | source)
XLA Modules:
  0.0 130.5 jit_solution(11523697200835841770)
XLA Ops:
  6.5 0.0 copy-start
  6.5 0.0 copy-start.4
  6.5 0.0 copy-start.3
  6.5 0.0 copy-start.2
  6.5 0.0 copy-start.1
  6.5 0.0 all-reduce.4.cloned.1.call-start
  6.6 0.9 copy.12
  7.5 0.1 reshape_squeeze.3
  7.6 0.7 convert_element_type.11
  8.3 0.1 dynamic_slice.3
  8.4 4.4 %fusion.2 = f32[8,8,3,128]{3,2,1,0:T(4,128)S(1)} fusion(f32[1,8,8,128,128]{4,3,2,1,0:T(8,128)} %param.8, f32[3,8,128,1]{2,1,0,3:T(8,128)S(1)} %bitcast.60), kind=kOutput, calls=%fused_computation.2 | convolution fusion | flops 37748736 | bytes 4304896 | tf_op jit(solution)/shard_map/tkn,kfnm->kftm/dot_general | solution.py:18
  12.8 0.9 fusion.8
  13.7 0.0 all-reduce.4.cloned.1.call-update
  13.8 0.0 copy-done
  13.8 0.7 convolution_bitcast_fusion
  14.5 19.9 %all_gather.3 = f32[16,8,2,256]{3,1,2,0:T(8,128)S(1)} all-gather(f32[1,8,2,256]{3,1,2,0:T(8,128)S(1)} %copy.15), channel_id=1, replica_groups=mesh['area'=16,'sec'=16] {'area'}, dimensions={0}, use_global_device_ids=true | all-gather | bytes 278528 | tf_op jit(solution)/shard_map/all_gather | solution.py:41
  34.4 0.0 copy-done.3
  34.4 0.3 fusion.6
  34.8 0.0 copy-done.4
  34.8 0.6 dynamic-slice
  36.1 86.3 %all-reduce.4.cloned.1.call-done = f32[128,384]{1,0:T(8,128)} async-done(((f32[128,384]{1,0:T(8,128)}), f32[128,384]{1,0:T(8,128)}) %all-reduce.4.cloned.1.call-update) | async-done | bytes 196624
  122.3 0.7 fusion.13
  123.0 0.0 copy-done.2
  123.0 0.0 copy-done.1
  123.0 0.6 fusion.17
  (6 shorter events, 0.0 us)
Async XLA Ops:
  6.5 7.2 %copy-start = (f32[1,8,2,128,128]{4,3,2,1,0:T(8,128)S(1)}, f32[1,8,2,128,128]{4,3,2,1,0:T(8,128)}, u32[]{:S(2)}) copy-start(f32[1,8,2,128,128]{4,3,2,1,0:T(8,128)} %param.10) | copy-start | bytes 3145732
  6.5 28.3 %copy-start.4 = (u32[256]{0:T(256)S(1)}, u32[256]{0:T(256)}, u32[]{:S(2)}) copy-start(u32[256]{0:T(256)} %constant.29) | copy-start | bytes 3076
  6.5 27.9 %copy-start.3 = (s32[16,1,2]{0,2,1:T(2,128)S(1)}, s32[16,1,2]{0,2,1:T(2,128)}, u32[]{:S(2)}) copy-start(s32[16,1,2]{0,2,1:T(2,128)} %param.11) | copy-start | bytes 388
  6.5 116.5 %copy-start.2 = (f32[1,1024]{1,0:T(1,128)S(1)}, f32[1,1024]{1,0:T(1,128)}, u32[]{:S(2)}) copy-start(f32[1,1024]{1,0:T(1,128)} %param.12) | copy-start | bytes 12292
  6.5 116.5 %copy-start.1 = (f32[1,1024]{1,0:T(1,128)S(1)}, f32[1,1024]{1,0:T(1,128)}, u32[]{:S(2)}) copy-start(f32[1,1024]{1,0:T(1,128)} %param.13) | copy-start | bytes 12292
  6.5 115.8 %all-reduce.4.cloned.1.call-start = ((), (), s32[]{:S(2)}) async-start(), calls=%async_computation | async-start | bytes 393216
Sparse Core Ops, SparseCore 0:
  13.9 108.4 all-reduce.3
where the time goes:
time: 131 us
  waiting for transfers between devices  86.3 us (66%)
  blocking collectives  19.9 us (15%)
  between operations  14.2 us (11%)
  matrix products  6.37 us (5%)
  other arithmetic  2.05 us (2%)
  local copies, waits for them, and re-layouts  1.68 us (1%)
    unnamed x2, waiting for transfers between devices  86.3 us
    all_gather x1, blocking collectives, body(): lax.all_gather(inter_part.reshape(1, blocks, fan_areas, later), 'area', a...  19.9 us
    dot_general x1, matrix products, body(): jnp.einsum('tkn,kfnm->kftm', spiking, intra_weight[0], precision=lax.Prec...  4.44 us
  transfers between devices with their start and end apart: 1, of which 1 were waited for; matrix products, arithmetic and copies ran while one was open for 1% of the time, Pallas kernels for 0%

commit v1 on v0

v1 whole, which is shorter than its diff:
```python
import functools

import jax
import jax.numpy as jnp
from jax import lax
from jax.experimental import pallas as pl
from jax.experimental.pallas import tpu as pltpu
from jax.sharding import PartitionSpec as P

MESH = pl.DeviceIdType.MESH
F32 = jnp.float32
BF16 = jnp.bfloat16


def split(values):
    high = values.astype(BF16)
    low = (values - high.astype(F32)).astype(BF16)
    return high, low


def kernel(
    areas, secs,
    spikes_ref, dest_ref, target_ref, v_ref, leak_ref, intra_ref, inter_ref,
    out_ref,
    intra_buf, inter_buf, intra_rows, inter_rows, intra_send, inter_send, intra_recv, inter_recv,
    load_sem, load_inter_sem, send_sem, recv_sem,
):
    steps, blocks, width = spikes_ref.shape
    fan = intra_ref.shape[1]
    fan_areas = inter_ref.shape[1]
    me_area = lax.axis_index("area")
    me_sec = lax.axis_index("sec")

    for k in range(blocks):
        pltpu.make_async_copy(intra_ref.at[k], intra_buf.at[k], load_sem.at[k]).start()
    load_inter = pltpu.make_async_copy(inter_ref, inter_buf, load_inter_sem)
    load_inter.start()

    barrier = pltpu.get_barrier_semaphore()
    for i in range(1, secs):
        pl.semaphore_signal(barrier, inc=1, device_id={"sec": lax.rem(me_sec + i, secs)}, device_id_type=MESH)
    for i in range(1, areas):
        pl.semaphore_signal(barrier, inc=1, device_id={"area": lax.rem(me_area + i, areas)}, device_id_type=MESH)

    lane = lax.broadcasted_iota(jnp.int32, (fan, width), 1)
    row = lax.broadcasted_iota(jnp.int32, (fan, width), 0)
    dest = pltpu.roll(dest_ref[...], lax.rem(width - me_sec * blocks, width), 1)
    dest = pltpu.roll(dest, 0, 1, stride=blocks, stride_axis=0)
    dest = jnp.sum(jnp.where(lane // blocks == row, dest, 0), axis=0, keepdims=True)
    half = fan * blocks
    dest = dest + pltpu.roll(dest, half, 1)
    grid_row = lax.broadcasted_iota(jnp.int32, (width, width), 0)
    picker = jnp.where(grid_row == dest, 1.0, 0.0).astype(BF16)

    def spikes_of(k):
        rows = spikes_ref[:, k, :].astype(F32).astype(BF16)
        rows = jnp.concatenate([rows, jnp.zeros((8 - steps, width), BF16)], axis=0)
        return jnp.concatenate([rows, rows], axis=1)

    for k in range(blocks):
        pltpu.make_async_copy(intra_ref.at[k], intra_buf.at[k], load_sem.at[k]).wait()
        lhs = spikes_of(k)
        for f in range(0, fan, 2):
            high, low = split(jnp.concatenate([intra_buf[k, f], intra_buf[k, f + 1]], axis=1))
            part = jnp.dot(lhs, jnp.concatenate([high, low], axis=0), preferred_element_type=F32)
            intra_rows[pl.ds((f * blocks + k) * 8, 8), :] = part[:, :width]
            intra_rows[pl.ds(((f + 1) * blocks + k) * 8, 8), :] = part[:, width:]

    for t in range(steps):
        high, low = split(intra_rows[pl.ds(t, half, stride=8), :])
        grid = jnp.dot(picker, jnp.concatenate([high, low], axis=0), preferred_element_type=F32)
        for p in range(secs):
            intra_send[p, t] = grid[p * blocks:(p + 1) * blocks, :]

    pl.semaphore_wait(barrier, secs - 1 + areas - 1)
    for i in range(1, secs):
        peer = lax.rem(me_sec + i, secs)
        pltpu.make_async_remote_copy(
            src_ref=intra_send.at[peer], dst_ref=intra_recv.at[i - 1],
            send_sem=send_sem.at[0], recv_sem=recv_sem.at[0],
            device_id={"sec": peer}, device_id_type=MESH,
        ).start()

    load_inter.wait()
    for k in range(blocks):
        lhs = spikes_of(k)
        high, low = split(jnp.concatenate([inter_buf[k, 0], inter_buf[k, 1]], axis=1))
        part = jnp.dot(lhs, jnp.concatenate([high, low], axis=0), preferred_element_type=F32)
        for j in range(fan_areas):
            inter_rows[j, pl.ds(k * 8, 8), :] = part[:, j * width:(j + 1) * width]
    for b in range(areas):
        for t in range(steps - 1):
            total = jnp.zeros((blocks, width), F32)
            for j in range(fan_areas):
                chosen = target_ref[j, me_area] == b
                total = jnp.where(chosen, inter_rows[j, pl.ds(t, blocks, stride=8), :], total)
            inter_send[b, t] = total
    for i in range(1, areas):
        peer = lax.rem(me_area + i, areas)
        pltpu.make_async_remote_copy(
            src_ref=inter_send.at[peer], dst_ref=inter_recv.at[i - 1],
            send_sem=send_sem.at[1], recv_sem=recv_sem.at[1],
            device_id={"area": peer}, device_id_type=MESH,
        ).start()

    pltpu.make_async_copy(inter_recv, inter_recv, recv_sem.at[1]).wait()
    inter_current = [inter_send[me_area, t] for t in range(steps - 1)]
    for i in range(areas - 1):
        inter_current = [inter_current[t] + inter_recv[i, t] for t in range(steps - 1)]
    pltpu.make_async_copy(intra_recv, intra_recv, recv_sem.at[0]).wait()
    current = [intra_send[me_sec, t] for t in range(steps)]
    for i in range(secs - 1):
        current = [current[t] + intra_recv[i, t] for t in range(steps)]

    potential = v_ref[...]
    for t in range(steps):
        potential = leak_ref[...] * potential * (1.0 - spikes_ref[t].astype(F32)) + current[t]
        if t > 0:
            potential = potential + inter_current[t - 1]
    out_ref[...] = potential

    pltpu.make_async_copy(inter_recv, inter_recv, send_sem.at[1]).wait()
    pltpu.make_async_copy(intra_recv, intra_recv, send_sem.at[0]).wait()


def body(areas, secs, spikes, intra_weight, intra_dest, inter_weight, inter_target, v_init, leak):
    _, blocks, fan, width, _ = intra_weight.shape
    fan_areas = inter_weight.shape[2]
    steps = spikes.shape[1]
    vmem = pl.BlockSpec(memory_space=pltpu.VMEM)
    smem = pl.BlockSpec(memory_space=pltpu.SMEM)
    anywhere = pl.BlockSpec(memory_space=pl.ANY)
    potential = pl.pallas_call(
        functools.partial(kernel, areas, secs),
        out_shape=jax.ShapeDtypeStruct((blocks, width), F32),
        in_specs=[vmem, vmem, smem, vmem, vmem, anywhere, anywhere],
        out_specs=vmem,
        scratch_shapes=[
            pltpu.VMEM((blocks, fan, width, width), F32),
            pltpu.VMEM((blocks, fan_areas, width, width), F32),
            pltpu.VMEM((fan * blocks * 8, width), F32),
            pltpu.VMEM((fan_areas, blocks * 8, width), F32),
            pltpu.VMEM((secs, steps, blocks, width), F32),
            pltpu.VMEM((areas, steps - 1, blocks, width), F32),
            pltpu.VMEM((secs - 1, steps, blocks, width), F32),
            pltpu.VMEM((areas - 1, steps - 1, blocks, width), F32),
            pltpu.SemaphoreType.DMA((blocks,)),
            pltpu.SemaphoreType.DMA,
            pltpu.SemaphoreType.DMA((2,)),
            pltpu.SemaphoreType.DMA((2,)),
        ],
        compiler_params=pltpu.CompilerParams(
            collective_id=0, has_side_effects=True, vmem_limit_bytes=60 << 20
        ),
    )(
        spikes.reshape(steps, blocks, width),
        intra_dest[0].T,
        inter_target[:, 0, :].T,
        v_init.reshape(blocks, width),
        leak.reshape(blocks, width),
        intra_weight[0],
        inter_weight[0],
    )
    return potential.reshape(1, blocks * width)


def solution(mesh):
    in_specs = (
        P("area", None, "sec"),
        P("area", "sec", None, None, None),
        P("area", None, None),
        P("area", "sec", None, None, None),
        P(None, "sec", None),
        P("area", "sec"),
        P("area", "sec"),
    )
    out_specs = P("area", "sec")
    run = functools.partial(body, mesh.shape["area"], mesh.shape["sec"])
    return jax.shard_map(run, mesh=mesh, in_specs=in_specs, out_specs=out_specs, check_vma=False)
```

time: 131 us -> 21.6 us (0.16)
  waiting for transfers between devices: 86.3 us -> 0 us
  Pallas kernels: 0 us -> 20.2 us
  blocking collectives: 19.9 us -> 0 us
  between operations: 14.2 us -> 0.01 us
  matrix products: 6.37 us -> 0 us
  other arithmetic: 2.05 us -> 0 us
    unnamed x2 -> x0, waiting for transfers between devices: 86.3 us -> none
    pallas_call x0 -> x1, Pallas kernels: none -> 20.2 us  [body(): pl.pallas_call(functools.partial(kernel, areas, secs), out_shape=jax.Shap...]
    all_gather x1 -> x0, blocking collectives: 19.9 us -> none  [body(): lax.all_gather(inter_part.reshape(1, blocks, fan_areas, later), 'area', a...]
    dot_general x4 -> x0, matrix products: 6.37 us -> none  [the longest x1 4.44 us: body(): jnp.einsum('tkn,kfnm->kftm', spiking, intra_weight[0], precision=lax.Prec...]
  transfers between devices with their start and end apart: 1 -> 0, of which waited for: 1 -> 0; matrix products, arithmetic and copies ran while one was open for 1% -> 0% of each run, Pallas kernels for 0% -> 0%
where the time goes in v1:
time: 21.6 us; the launch traced here: 21.4 us
  Pallas kernels  20.2 us (94%)
  local copies, waits for them, and re-layouts  1.28 us (6%)
    pallas_call x1, Pallas kernels, body(): pl.pallas_call(functools.partial(kernel, areas, secs), out_shape=jax.Shap...  20.2 us
    unnamed x1, local copies, waits for them, and re-layouts  1.28 us

profile of v1, /device:TPU:1, one launch (start us, length us, event | category | flops | bytes accessed | tf_op | source)
XLA Modules:
  0.0 21.4 jit_solution(17670397374019914771)
XLA Ops:
  0.0 20.2 %shard_map.73 = f32[8,128]{1,0:T(8,128)} custom-call(s32[3,8,128]{2,1,0:T(8,128)} %bitcast.15, s32[8,128]{1,0:T(8,128)} %bitcast.16, s32[2,16]{1,0:T(2,128)} %bitcast.19, f32[8,128]{1,0:T(8,128)} %bitcast.17, f32[8,128]{1,0:T(8,128)} %bitcast.18, f32[8,8,128,128]{3,2,1,0:T(8,128)} %bitcast.12, f32[8,2,128,128]{3,2,1,0:T(8,128)} %bitcast.13), custom_call_target="tpu_custom_call" | custom-call | tf_op jit(solution)/shard_map/pallas_call | solution.py:133
  20.2 1.3 %copy.9 = f32[1,1024]{1,0:T(1,128)} copy(f32[1,1024]{1,0:T(1,128)} %bitcast.14) | data formatting | bytes 8192

commit v2 on v1

v2 whole, which is shorter than its diff:
```python
import functools

import jax
import jax.numpy as jnp
from jax import lax
from jax.experimental import pallas as pl
from jax.experimental.pallas import tpu as pltpu
from jax.sharding import PartitionSpec as P

MESH = pl.DeviceIdType.MESH
F32 = jnp.float32
BF16 = jnp.bfloat16
SIDE = 4
CORES = 2


def split(values):
    high = values.astype(BF16)
    low = (values - high.astype(F32)).astype(BF16)
    return high, low


def kernel(
    spikes_hbm, dest_hbm, target_hbm, v_hbm, leak_hbm, intra_hbm, inter_hbm,
    out_ref,
    spikes_ref, dest_ref, target_ref, v_ref, leak_ref, intra_buf, inter_buf,
    intra_rows, inter_rows, intra_send, sib_recv, z_send, z_recv,
    x_send, x_recv, y_send, y_recv,
    small_sem, load_sem, send_sem, recv_sem,
):
    steps, blocks, width = spikes_ref.shape
    fan = intra_buf.shape[1]
    fan_areas = inter_buf.shape[1]
    chips = z_send.shape[0]
    later = steps - 1
    me_area = lax.axis_index("area")
    me_sec = lax.axis_index("sec")
    x, y = me_area // SIDE, me_area % SIDE
    z, core = me_sec // CORES, me_sec % CORES

    def at(dx=0, dy=0, dz=0, other=False):
        area = lax.rem(x + dx, SIDE) * SIDE + lax.rem(y + dy, SIDE)
        sec = lax.rem(z + dz, chips) * CORES + (1 - core if other else core)
        return {"area": area, "sec": sec}

    peers = [at(dz=d) for d in sorted(range(1, chips), key=lambda d: -min(d, chips - d))]
    peers += [at(dx=d) for d in (2, 1, 3)] + [at(dy=d) for d in (2, 1, 3)] + [at(other=True)]

    def small(i):
        src = (spikes_hbm, dest_hbm, target_hbm, v_hbm, leak_hbm)[i]
        dst = (spikes_ref, dest_ref, target_ref, v_ref, leak_ref)[i]
        return pltpu.make_async_copy(src, dst, small_sem.at[i])

    def load(k):
        if k == blocks:
            return pltpu.make_async_copy(inter_hbm, inter_buf, load_sem.at[k])
        return pltpu.make_async_copy(intra_hbm.at[k], intra_buf.at[k], load_sem.at[k])

    for i in range(3):
        small(i).start()
    load(blocks).start()
    for k in range(blocks):
        load(k).start()
    barrier = pltpu.get_barrier_semaphore()
    for peer in peers:
        pl.semaphore_signal(barrier, inc=1, device_id=peer, device_id_type=MESH)
    for i in range(3, 5):
        small(i).start()

    for i in range(3):
        small(i).wait()
    lane = lax.broadcasted_iota(jnp.int32, (fan, width), 1)
    row = lax.broadcasted_iota(jnp.int32, (fan, width), 0)
    dest = pltpu.roll(dest_ref[...], lax.rem(width - me_sec * blocks, width), 1)
    dest = pltpu.roll(dest, 0, 1, stride=blocks, stride_axis=0)
    dest = jnp.sum(jnp.where(lane // blocks == row, dest, 0), axis=0, keepdims=True)
    half = fan * blocks
    dest = dest + pltpu.roll(dest, half, 1)
    grid_row = lax.broadcasted_iota(jnp.int32, (width, width), 0)
    picker = jnp.where(grid_row == dest, 1.0, 0.0).astype(BF16)
    target_lane = lax.broadcasted_iota(jnp.int32, target_ref.shape, 1)
    target = jnp.sum(jnp.where(target_lane == me_area, target_ref[...], 0), axis=1, keepdims=True)
    targets = [jnp.broadcast_to(target[j:j + 1], (blocks, width)) for j in range(fan_areas)]

    def spikes_of(k):
        rows = spikes_ref[:, k, :].astype(F32).astype(BF16)
        rows = jnp.concatenate([rows, jnp.zeros((8 - steps, width), BF16)], axis=0)
        return jnp.concatenate([rows, rows], axis=1)

    def products(k, left, right):
        high, low = split(jnp.concatenate([left, right], axis=1))
        rhs = jnp.concatenate([high, low], axis=0)
        part = jnp.dot(spikes_of(k), rhs, preferred_element_type=F32)
        return part[:, :width], part[:, width:]

    load(blocks).wait()
    for k in range(blocks):
        parts = products(k, inter_buf[k, 0], inter_buf[k, 1])
        for j in range(fan_areas):
            inter_rows[j, pl.ds(k * 8, 8), :] = parts[j]
    for t in range(later):
        rows = [inter_rows[j, pl.ds(t, blocks, stride=8), :] for j in range(fan_areas)]
        for b in range(SIDE * SIDE):
            total = jnp.where(targets[0] == b, rows[0], 0.0)
            for j in range(1, fan_areas):
                total = jnp.where(targets[j] == b, rows[j], total)
            x_send[b // SIDE, b % SIDE, t] = total

    for k in range(blocks):
        load(k).wait()
        for f in range(0, fan, 2):
            left, right = products(k, intra_buf[k, f], intra_buf[k, f + 1])
            intra_rows[pl.ds((f * blocks + k) * 8, 8), :] = left
            intra_rows[pl.ds(((f + 1) * blocks + k) * 8, 8), :] = right
    for t in range(steps):
        high, low = split(intra_rows[pl.ds(t, half, stride=8), :])
        grid = jnp.dot(picker, jnp.concatenate([high, low], axis=0), preferred_element_type=F32)
        for p in range(chips * CORES):
            intra_send[p % CORES, p // CORES, t] = grid[p * blocks:(p + 1) * blocks, :]

    def remote(i, src, dst, peer):
        return pltpu.make_async_remote_copy(
            src_ref=src, dst_ref=dst, send_sem=send_sem.at[i], recv_sem=recv_sem.at[i],
            device_id=peer, device_id_type=MESH,
        )

    def wait(sem, i, ref):
        pltpu.make_async_copy(ref, ref, sem.at[i]).wait()

    pl.semaphore_wait(barrier, len(peers))
    remote(0, intra_send.at[1 - core], sib_recv, at(other=True)).start()
    for d in (2, 1, 3):
        remote(1, x_send.at[lax.rem(x + d, SIDE)], x_recv.at[d - 1], at(dx=d)).start()

    wait(recv_sem, 0, sib_recv)
    for p in range(chips):
        for t in range(steps):
            z_send[p, t] = intra_send[core, p, t] + sib_recv[p, t]
    for d in sorted(range(1, chips), key=lambda d: -min(d, chips - d)):
        remote(2, z_send.at[lax.rem(z + d, chips)], z_recv.at[d - 1], at(dz=d)).start()

    wait(recv_sem, 1, x_recv)
    for b in range(SIDE):
        for t in range(later):
            y_send[b, t] = x_send[x, b, t] + x_recv[0, b, t] + x_recv[1, b, t] + x_recv[2, b, t]
    for d in (2, 1, 3):
        remote(3, y_send.at[lax.rem(y + d, SIDE)], y_recv.at[d - 1], at(dy=d)).start()

    for i in range(3, 5):
        small(i).wait()
    wait(recv_sem, 2, z_recv)
    current = [z_send[z, t] for t in range(steps)]
    for i in range(chips - 1):
        current = [current[t] + z_recv[i, t] for t in range(steps)]
    wait(recv_sem, 3, y_recv)
    for t in range(later):
        extra = y_send[y, t]
        for i in range(SIDE - 1):
            extra = extra + y_recv[i, t]
        current[t + 1] = current[t + 1] + extra

    potential = v_ref[...]
    for t in range(steps):
        potential = leak_ref[...] * potential * (1.0 - spikes_ref[t].astype(F32)) + current[t]
    out_ref[...] = potential

    wait(send_sem, 0, sib_recv)
    wait(send_sem, 1, x_recv)
    wait(send_sem, 2, z_recv)
    wait(send_sem, 3, y_recv)


def body(areas, secs, spikes, intra_weight, intra_dest, inter_weight, inter_target, v_init, leak):
    _, blocks, fan, width, _ = intra_weight.shape
    fan_areas = inter_weight.shape[2]
    steps = spikes.shape[1]
    chips = secs // CORES
    assert areas == SIDE * SIDE
    hbm = pl.BlockSpec(memory_space=pl.ANY)
    tile = (blocks, width)
    potential = pl.pallas_call(
        kernel,
        out_shape=jax.ShapeDtypeStruct(tile, F32),
        in_specs=[hbm] * 7,
        out_specs=pl.BlockSpec(memory_space=pltpu.VMEM),
        scratch_shapes=[
            pltpu.VMEM((steps,) + tile, jnp.int32),
            pltpu.VMEM((fan, width), jnp.int32),
            pltpu.VMEM((fan_areas, areas), jnp.int32),
            pltpu.VMEM(tile, F32),
            pltpu.VMEM(tile, F32),
            pltpu.VMEM((blocks, fan, width, width), F32),
            pltpu.VMEM((blocks, fan_areas, width, width), F32),
            pltpu.VMEM((fan * blocks * 8, width), F32),
            pltpu.VMEM((fan_areas, blocks * 8, width), F32),
            pltpu.VMEM((CORES, chips, steps) + tile, F32),
            pltpu.VMEM((chips, steps) + tile, F32),
            pltpu.VMEM((chips, steps) + tile, F32),
            pltpu.VMEM((chips - 1, steps) + tile, F32),
            pltpu.VMEM((SIDE, SIDE, steps - 1) + tile, F32),
            pltpu.VMEM((SIDE - 1, SIDE, steps - 1) + tile, F32),
            pltpu.VMEM((SIDE, steps - 1) + tile, F32),
            pltpu.VMEM((SIDE - 1, steps - 1) + tile, F32),
            pltpu.SemaphoreType.DMA((5,)),
            pltpu.SemaphoreType.DMA((blocks + 1,)),
            pltpu.SemaphoreType.DMA((4,)),
            pltpu.SemaphoreType.DMA((4,)),
        ],
        compiler_params=pltpu.CompilerParams(
            collective_id=0, has_side_effects=True, vmem_limit_bytes=60 << 20
        ),
    )(
        spikes.reshape((steps,) + tile),
        intra_dest[0].T,
        inter_target[:, 0, :].T,
        v_init.reshape(tile),
        leak.reshape(tile),
        intra_weight[0],
        inter_weight[0],
    )
    return potential.reshape(1, blocks * width)


def solution(mesh):
    in_specs = (
        P("area", None, "sec"),
        P("area", "sec", None, None, None),
        P("area", None, None),
        P("area", "sec", None, None, None),
        P(None, "sec", None),
        P("area", "sec"),
        P("area", "sec"),
    )
    out_specs = P("area", "sec")
    run = functools.partial(body, mesh.shape["area"], mesh.shape["sec"])
    return jax.shard_map(run, mesh=mesh, in_specs=in_specs, out_specs=out_specs, check_vma=False)
```

time: 21.6 us -> 18.3 us (0.85)
  the two profiles are of different devices: /device:TPU:1 before, /device:TPU:8 now
where the time goes in v2:
time: 18.3 us; the launch traced here: 18.2 us
  Pallas kernels  16.9 us (92%)
  local copies, waits for them, and re-layouts  1.28 us (7%)
    pallas_call x1, Pallas kernels, body(): pl.pallas_call(kernel, out_shape=jax.ShapeDtypeStruct(tile, F32), in_spec...  16.9 us
    unnamed x1, local copies, waits for them, and re-layouts  1.28 us

profile of v2, /device:TPU:8, one launch (start us, length us, event | category | flops | bytes accessed | tf_op | source)
XLA Modules:
  0.0 18.2 jit_solution(1564021726067681308)
XLA Ops:
  0.0 16.9 %shard_map.73 = f32[8,128]{1,0:T(8,128)} custom-call(s32[3,8,128]{2,1,0:T(8,128)} %bitcast.15, s32[8,128]{1,0:T(8,128)} %bitcast.16, s32[2,16]{1,0:T(2,128)} %bitcast.19, f32[8,128]{1,0:T(8,128)} %bitcast.17, f32[8,128]{1,0:T(8,128)} %bitcast.18, f32[8,8,128,128]{3,2,1,0:T(8,128)} %bitcast.12, f32[8,2,128,128]{3,2,1,0:T(8,128)} %bitcast.13), custom_call_target="tpu_custom_call" | custom-call | tf_op jit(solution)/shard_map/pallas_call | solution.py:181
  16.9 1.3 %copy.9 = f32[1,1024]{1,0:T(1,128)} copy(f32[1,1024]{1,0:T(1,128)} %bitcast.14) | data formatting | bytes 8192

commit v3 on v2

--- a/solution.py
+++ b/solution.py
@@ -22,11 +22,11 @@
 
 def kernel(
     spikes_hbm, dest_hbm, target_hbm, v_hbm, leak_hbm, intra_hbm, inter_hbm,
-    out_ref,
+    held_ref, last_ref,
     spikes_ref, dest_ref, target_ref, v_ref, leak_ref, intra_buf, inter_buf,
     intra_rows, inter_rows, intra_send, sib_recv, z_send, z_recv,
     x_send, x_recv, y_send, y_recv,
-    small_sem, load_sem, send_sem, recv_sem,
+    small_sem, load_sem, send_sem, recv_sem, ready_sem,
 ):
     steps, blocks, width = spikes_ref.shape
     fan = intra_buf.shape[1]
@@ -43,8 +43,21 @@
         sec = lax.rem(z + dz, chips) * CORES + (1 - core if other else core)
         return {"area": area, "sec": sec}
 
-    peers = [at(dz=d) for d in sorted(range(1, chips), key=lambda d: -min(d, chips - d))]
-    peers += [at(dx=d) for d in (2, 1, 3)] + [at(dy=d) for d in (2, 1, 3)] + [at(other=True)]
+    far_z = sorted(range(1, chips), key=lambda d: -min(d, chips - d))
+    axes = (
+        (z, chips, far_z, lambda d: at(dz=d)),
+        (x, SIDE, (2, 1, 3), lambda d: at(dx=d)),
+        (y, SIDE, (2, 1, 3), lambda d: at(dy=d)),
+    )
+
+    def partners(axis, after, act):
+        place, length, distances, peer = axes[axis]
+        for d in distances:
+            follows = place + d < length
+
+            @pl.when(follows if after else jnp.logical_not(follows))
+            def _():
+                act(d, peer(d))
 
     def small(i):
         src = (spikes_hbm, dest_hbm, target_hbm, v_hbm, leak_hbm)[i]
@@ -55,6 +68,31 @@
         if k == blocks:
             return pltpu.make_async_copy(inter_hbm, inter_buf, load_sem.at[k])
         return pltpu.make_async_copy(intra_hbm.at[k], intra_buf.at[k], load_sem.at[k])
+
+    def remote(i, src, dst, peer):
+        return pltpu.make_async_remote_copy(
+            src_ref=src, dst_ref=dst, send_sem=send_sem.at[i], recv_sem=recv_sem.at[i],
+            device_id=peer, device_id_type=MESH,
+        )
+
+    def wait(sem, i, ref):
+        pltpu.make_async_copy(ref, ref, sem.at[i]).wait()
+
+    def send_x(d, peer):
+        remote(1, x_send.at[lax.rem(x + d, SIDE)], x_recv.at[d - 1], peer).start()
+
+    def send_z(d, peer):
+        remote(2, z_send.at[lax.rem(z + d, chips)], z_recv.at[d - 1], peer).start()
+
+    def send_y(d, peer):
+        remote(3, y_send.at[lax.rem(y + d, SIDE)], y_recv.at[d - 1], peer).start()
+
+    def entered(axis):
+        place, length, _, _ = axes[axis]
+
+        @pl.when(place < length - 1)
+        def _():
+            pl.semaphore_wait(ready_sem.at[axis], length - 1 - place)
 
     for i in range(3):
         small(i).start()
@@ -62,8 +100,9 @@
     for k in range(blocks):
         load(k).start()
     barrier = pltpu.get_barrier_semaphore()
-    for peer in peers:
-        pl.semaphore_signal(barrier, inc=1, device_id=peer, device_id_type=MESH)
+    for axis in range(3):
+        partners(axis, True, lambda d, peer: pl.semaphore_signal(barrier, inc=1, device_id=peer, device_id_type=MESH))
+    pl.semaphore_signal(barrier, inc=1, device_id=at(other=True), device_id_type=MESH)
     for i in range(3, 5):
         small(i).start()
 
@@ -93,7 +132,13 @@
         part = jnp.dot(spikes_of(k), rhs, preferred_element_type=F32)
         return part[:, :width], part[:, width:]
 
-    load(blocks).wait()
+    pl.semaphore_wait(barrier, 1 + x + y + z)
+    for axis in range(3):
+        ready = ready_sem.at[axis]
+        partners(axis, False, lambda d, peer: pl.semaphore_signal(ready, inc=1, device_id=peer, device_id_type=MESH))
+
+    for k in [blocks] + list(range(blocks // 2)):
+        load(k).wait()
     for k in range(blocks):
         parts = products(k, inter_buf[k, 0], inter_buf[k, 1])
         for j in range(fan_areas):
@@ -106,45 +151,46 @@
                 total = jnp.where(targets[j] == b, rows[j], total)
             x_send[b // SIDE, b % SIDE, t] = total
 
-    for k in range(blocks):
-        load(k).wait()
+    def intra(k):
         for f in range(0, fan, 2):
             left, right = products(k, intra_buf[k, f], intra_buf[k, f + 1])
             intra_rows[pl.ds((f * blocks + k) * 8, 8), :] = left
             intra_rows[pl.ds(((f + 1) * blocks + k) * 8, 8), :] = right
+
+    for k in range(blocks // 2):
+        intra(k)
+    partners(1, False, send_x)
+
+
+    for k in range(blocks // 2, blocks):
+        load(k).wait()
+    for k in range(blocks // 2, blocks):
+        intra(k)
     for t in range(steps):
         high, low = split(intra_rows[pl.ds(t, half, stride=8), :])
         grid = jnp.dot(picker, jnp.concatenate([high, low], axis=0), preferred_element_type=F32)
         for p in range(chips * CORES):
             intra_send[p % CORES, p // CORES, t] = grid[p * blocks:(p + 1) * blocks, :]
 
-    def remote(i, src, dst, peer):
-        return pltpu.make_async_remote_copy(
-            src_ref=src, dst_ref=dst, send_sem=send_sem.at[i], recv_sem=recv_sem.at[i],
-            device_id=peer, device_id_type=MESH,
-        )
-
-    def wait(sem, i, ref):
-        pltpu.make_async_copy(ref, ref, sem.at[i]).wait()
-
-    pl.semaphore_wait(barrier, len(peers))
     remote(0, intra_send.at[1 - core], sib_recv, at(other=True)).start()
-    for d in (2, 1, 3):
-        remote(1, x_send.at[lax.rem(x + d, SIDE)], x_recv.at[d - 1], at(dx=d)).start()
 
     wait(recv_sem, 0, sib_recv)
     for p in range(chips):
         for t in range(steps):
             z_send[p, t] = intra_send[core, p, t] + sib_recv[p, t]
-    for d in sorted(range(1, chips), key=lambda d: -min(d, chips - d)):
-        remote(2, z_send.at[lax.rem(z + d, chips)], z_recv.at[d - 1], at(dz=d)).start()
+    partners(0, False, send_z)
+    entered(1)
+    partners(1, True, send_x)
 
     wait(recv_sem, 1, x_recv)
     for b in range(SIDE):
         for t in range(later):
             y_send[b, t] = x_send[x, b, t] + x_recv[0, b, t] + x_recv[1, b, t] + x_recv[2, b, t]
-    for d in (2, 1, 3):
-        remote(3, y_send.at[lax.rem(y + d, SIDE)], y_recv.at[d - 1], at(dy=d)).start()
+    partners(2, False, send_y)
+    entered(0)
+    partners(0, True, send_z)
+    entered(2)
+    partners(2, True, send_y)
 
     for i in range(3, 5):
         small(i).wait()
@@ -160,9 +206,10 @@
         current[t + 1] = current[t + 1] + extra
 
     potential = v_ref[...]
-    for t in range(steps):
+    for t in range(later):
         potential = leak_ref[...] * potential * (1.0 - spikes_ref[t].astype(F32)) + current[t]
-    out_ref[...] = potential
+    held_ref[...] = leak_ref[...] * potential * (1.0 - spikes_ref[later].astype(F32))
+    last_ref[...] = current[later]
 
     wait(send_sem, 0, sib_recv)
     wait(send_sem, 1, x_recv)
@@ -176,13 +223,13 @@
     steps = spikes.shape[1]
     chips = secs // CORES
     assert areas == SIDE * SIDE
-    hbm = pl.BlockSpec(memory_space=pl.ANY)
+    hbm = pl.BlockSpec(memory_space=pltpu.HBM)
     tile = (blocks, width)
-    potential = pl.pallas_call(
+    held, last = pl.pallas_call(
         kernel,
-        out_shape=jax.ShapeDtypeStruct(tile, F32),
+        out_shape=[jax.ShapeDtypeStruct(tile, F32)] * 2,
         in_specs=[hbm] * 7,
-        out_specs=pl.BlockSpec(memory_space=pltpu.VMEM),
+        out_specs=[pl.BlockSpec(memory_space=pltpu.VMEM)] * 2,
         scratch_shapes=[
             pltpu.VMEM((steps,) + tile, jnp.int32),
             pltpu.VMEM((fan, width), jnp.int32),
@@ -205,20 +252,24 @@
             pltpu.SemaphoreType.DMA((blocks + 1,)),
             pltpu.SemaphoreType.DMA((4,)),
             pltpu.SemaphoreType.DMA((4,)),
+            pltpu.SemaphoreType.REGULAR((3,)),
         ],
         compiler_params=pltpu.CompilerParams(
-            collective_id=0, has_side_effects=True, vmem_limit_bytes=60 << 20
+            collective_id=0, has_side_effects=True, vmem_limit_bytes=16 << 20
         ),
-    )(
-        spikes.reshape((steps,) + tile),
-        intra_dest[0].T,
-        inter_target[:, 0, :].T,
-        v_init.reshape(tile),
-        leak.reshape(tile),
-        intra_weight[0],
-        inter_weight[0],
-    )
-    return potential.reshape(1, blocks * width)
+    )(*(
+        pltpu.with_memory_space_constraint(operand, pltpu.HBM)
+        for operand in (
+            spikes.reshape((steps,) + tile),
+            intra_dest[0].T,
+            inter_target[:, 0, :].T,
+            v_init.reshape(tile),
+            leak.reshape(tile),
+            intra_weight[0],
+            inter_weight[0],
+        )
+    ))
+    return (held + last).reshape(1, blocks * width)
 
 
 def solution(mesh):

time: 18.3 us -> 15.7 us (0.86)
  the two profiles are of different devices: /device:TPU:8 before, /device:TPU:1 now
where the time goes in v3:
time: 15.7 us; the launch traced here: 15.6 us
  Pallas kernels  15 us (96%)
  other arithmetic  0.6 us (4%)
    pallas_call x1, Pallas kernels, body(): pl.pallas_call(kernel, out_shape=[jax.ShapeDtypeStruct(tile, F32)] * 2, i...  15 us
    add x1, other arithmetic, body(): return (held + last).reshape(1, blocks * width)  0.6 us

profile of v3, /device:TPU:1, one launch (start us, length us, event | category | flops | bytes accessed | tf_op | source)
XLA Modules:
  0.0 15.6 jit_solution(3714808431933585763)
XLA Ops:
  0.0 15.0 %shard_map.73 = (f32[8,128]{1,0:T(8,128)S(1)}, f32[8,128]{1,0:T(8,128)S(1)}) custom-call(s32[3,8,128]{2,1,0:T(8,128)} %bitcast.14, s32[8,128]{1,0:T(8,128)} %bitcast.15, s32[2,16]{1,0:T(2,128)} %bitcast.18, f32[8,128]{1,0:T(8,128)} %bitcast.16, f32[8,128]{1,0:T(8,128)} %bitcast.17, f32[8,8,128,128]{3,2,1,0:T(8,128)} %bitcast.12, f32[8,2,128,128]{3,2,1,0:T(8,128)} %bitcast.13), custom_call_target="tpu_custom_call" | custom-call | tf_op jit(solution)/shard_map/pallas_call | solution.py:228
  15.0 0.6 %add.3 = f32[8,128]{1,0:T(8,128)} add(f32[8,128]{1,0:T(8,128)S(1)} %get-tuple-element.7, f32[8,128]{1,0:T(8,128)S(1)} %get-tuple-element.8) | non-fusion elementwise | flops 1024 | bytes 12288 | tf_op jit(solution)/shard_map/add | solution.py:272

commit v4 on v3

--- a/solution.py
+++ b/solution.py
@@ -11,6 +11,7 @@
 F32 = jnp.float32
 BF16 = jnp.bfloat16
 SIDE = 4
+HALVES = 2
 CORES = 2
 
 
@@ -52,7 +53,7 @@
 
     def partners(axis, after, act):
         place, length, distances, peer = axes[axis]
-        for d in distances:
+        for d in distances if after else sorted(distances):
             follows = place + d < length
 
             @pl.when(follows if after else jnp.logical_not(follows))
@@ -65,9 +66,10 @@
         return pltpu.make_async_copy(src, dst, small_sem.at[i])
 
     def load(k):
-        if k == blocks:
+        if k == HALVES:
             return pltpu.make_async_copy(inter_hbm, inter_buf, load_sem.at[k])
-        return pltpu.make_async_copy(intra_hbm.at[k], intra_buf.at[k], load_sem.at[k])
+        half = pl.ds(k * (blocks // HALVES), blocks // HALVES)
+        return pltpu.make_async_copy(intra_hbm.at[half], intra_buf.at[half], load_sem.at[k])
 
     def remote(i, src, dst, peer):
         return pltpu.make_async_remote_copy(
@@ -94,17 +96,21 @@
         def _():
             pl.semaphore_wait(ready_sem.at[axis], length - 1 - place)
 
+    for k in (HALVES, 0, 1):
+        load(k).start()
     for i in range(3):
         small(i).start()
-    load(blocks).start()
-    for k in range(blocks):
-        load(k).start()
     barrier = pltpu.get_barrier_semaphore()
     for axis in range(3):
         partners(axis, True, lambda d, peer: pl.semaphore_signal(barrier, inc=1, device_id=peer, device_id_type=MESH))
     pl.semaphore_signal(barrier, inc=1, device_id=at(other=True), device_id_type=MESH)
     for i in range(3, 5):
         small(i).start()
+
+    pl.semaphore_wait(barrier, 1 + x + y + z)
+    for axis in range(3):
+        ready = ready_sem.at[axis]
+        partners(axis, False, lambda d, peer: pl.semaphore_signal(ready, inc=1, device_id=peer, device_id_type=MESH))
 
     for i in range(3):
         small(i).wait()
@@ -132,13 +138,8 @@
         part = jnp.dot(spikes_of(k), rhs, preferred_element_type=F32)
         return part[:, :width], part[:, width:]
 
-    pl.semaphore_wait(barrier, 1 + x + y + z)
-    for axis in range(3):
-        ready = ready_sem.at[axis]
-        partners(axis, False, lambda d, peer: pl.semaphore_signal(ready, inc=1, device_id=peer, device_id_type=MESH))
-
-    for k in [blocks] + list(range(blocks // 2)):
-        load(k).wait()
+    load(HALVES).wait()
+    load(0).wait()
     for k in range(blocks):
         parts = products(k, inter_buf[k, 0], inter_buf[k, 1])
         for j in range(fan_areas):
@@ -159,11 +160,9 @@
 
     for k in range(blocks // 2):
         intra(k)
+
     partners(1, False, send_x)
-
-
-    for k in range(blocks // 2, blocks):
-        load(k).wait()
+    load(1).wait()
     for k in range(blocks // 2, blocks):
         intra(k)
     for t in range(steps):
@@ -173,6 +172,7 @@
             intra_send[p % CORES, p // CORES, t] = grid[p * blocks:(p + 1) * blocks, :]
 
     remote(0, intra_send.at[1 - core], sib_recv, at(other=True)).start()
+
 
     wait(recv_sem, 0, sib_recv)
     for p in range(chips):
@@ -194,16 +194,16 @@
 
     for i in range(3, 5):
         small(i).wait()
-    wait(recv_sem, 2, z_recv)
+    wait(recv_sem, 3, y_recv)
     current = [z_send[z, t] for t in range(steps)]
-    for i in range(chips - 1):
-        current = [current[t] + z_recv[i, t] for t in range(steps)]
-    wait(recv_sem, 3, y_recv)
     for t in range(later):
         extra = y_send[y, t]
         for i in range(SIDE - 1):
             extra = extra + y_recv[i, t]
         current[t + 1] = current[t + 1] + extra
+    wait(recv_sem, 2, z_recv)
+    for i in range(chips - 1):
+        current = [current[t] + z_recv[i, t] for t in range(steps)]
 
     potential = v_ref[...]
     for t in range(later):
@@ -249,7 +249,7 @@
             pltpu.VMEM((SIDE, steps - 1) + tile, F32),
             pltpu.VMEM((SIDE - 1, steps - 1) + tile, F32),
             pltpu.SemaphoreType.DMA((5,)),
-            pltpu.SemaphoreType.DMA((blocks + 1,)),
+            pltpu.SemaphoreType.DMA((HALVES + 1,)),
             pltpu.SemaphoreType.DMA((4,)),
             pltpu.SemaphoreType.DMA((4,)),
             pltpu.SemaphoreType.REGULAR((3,)),

time: 15.7 us -> 15.2 us (0.968)
  Pallas kernels: 15 us -> 14.5 us
    pallas_call x1, Pallas kernels: 15 us -> 14.5 us  [body(): pl.pallas_call(kernel, out_shape=[jax.ShapeDtypeStruct(tile, F32)] * 2, i...]
where the time goes in v4:
time: 15.2 us; the launch traced here: 15.1 us
  Pallas kernels  14.5 us (95%)
  other arithmetic  0.6 us (4%)
    pallas_call x1, Pallas kernels, body(): pl.pallas_call(kernel, out_shape=[jax.ShapeDtypeStruct(tile, F32)] * 2, i...  14.5 us
    add x1, other arithmetic, body(): return (held + last).reshape(1, blocks * width)  0.6 us

profile of v4, /device:TPU:1, one launch (start us, length us, event | category | flops | bytes accessed | tf_op | source)
XLA Modules:
  0.0 15.1 jit_solution(13758725590402556331)
XLA Ops:
  0.0 14.5 %shard_map.73 = (f32[8,128]{1,0:T(8,128)S(1)}, f32[8,128]{1,0:T(8,128)S(1)}) custom-call(s32[3,8,128]{2,1,0:T(8,128)} %bitcast.14, s32[8,128]{1,0:T(8,128)} %bitcast.15, s32[2,16]{1,0:T(2,128)} %bitcast.18, f32[8,128]{1,0:T(8,128)} %bitcast.16, f32[8,128]{1,0:T(8,128)} %bitcast.17, f32[8,8,128,128]{3,2,1,0:T(8,128)} %bitcast.12, f32[8,2,128,128]{3,2,1,0:T(8,128)} %bitcast.13), custom_call_target="tpu_custom_call" | custom-call | tf_op jit(solution)/shard_map/pallas_call | solution.py:228
  14.5 0.6 %add.3 = f32[8,128]{1,0:T(8,128)} add(f32[8,128]{1,0:T(8,128)S(1)} %get-tuple-element.7, f32[8,128]{1,0:T(8,128)S(1)} %get-tuple-element.8) | non-fusion elementwise | flops 1024 | bytes 12288 | tf_op jit(solution)/shard_map/add | solution.py:272

commit v5 on v4

--- a/solution.py
+++ b/solution.py
@@ -44,6 +44,9 @@
         sec = lax.rem(z + dz, chips) * CORES + (1 - core if other else core)
         return {"area": area, "sec": sec}
 
+    late = chips // 2
+    is_late = z >= late
+
     far_z = sorted(range(1, chips), key=lambda d: -min(d, chips - d))
     axes = (
         (z, chips, far_z, lambda d: at(dz=d)),
@@ -96,7 +99,7 @@
         def _():
             pl.semaphore_wait(ready_sem.at[axis], length - 1 - place)
 
-    for k in (HALVES, 0, 1):
+    for k in range(HALVES + 1):
         load(k).start()
     for i in range(3):
         small(i).start()
@@ -104,10 +107,16 @@
     for axis in range(3):
         partners(axis, True, lambda d, peer: pl.semaphore_signal(barrier, inc=1, device_id=peer, device_id_type=MESH))
     pl.semaphore_signal(barrier, inc=1, device_id=at(other=True), device_id_type=MESH)
+
+    @pl.when(z == 0)
+    def _():
+        for d in range(late, chips):
+            pl.semaphore_signal(barrier, inc=1, device_id=at(dz=d, other=True), device_id_type=MESH)
+
     for i in range(3, 5):
         small(i).start()
 
-    pl.semaphore_wait(barrier, 1 + x + y + z)
+    pl.semaphore_wait(barrier, 1 + x + y + z + z // late)
     for axis in range(3):
         ready = ready_sem.at[axis]
         partners(axis, False, lambda d, peer: pl.semaphore_signal(ready, inc=1, device_id=peer, device_id_type=MESH))
@@ -138,8 +147,35 @@
         part = jnp.dot(spikes_of(k), rhs, preferred_element_type=F32)
         return part[:, :width], part[:, width:]
 
+    def intra(k):
+        for f in range(0, fan, 2):
+            left, right = products(k, intra_buf[k, f], intra_buf[k, f + 1])
+            intra_rows[pl.ds((f * blocks + k) * 8, 8), :] = left
+            intra_rows[pl.ds(((f + 1) * blocks + k) * 8, 8), :] = right
+
+    load(0).wait()
+    for k in range(blocks // 2):
+        intra(k)
+
+    load(1).wait()
+    for k in range(blocks // 2, blocks):
+        intra(k)
+    for t in range(steps):
+        high, low = split(intra_rows[pl.ds(t, half, stride=8), :])
+        grid = jnp.dot(picker, jnp.concatenate([high, low], axis=0), preferred_element_type=F32)
+        for p in range(chips * CORES):
+            intra_send[p % CORES, p // CORES, t] = grid[p * blocks:(p + 1) * blocks, :]
+
+
+    @pl.when(is_late)
+    def _():
+        back = chips - z
+        remote(2, intra_send.at[core, 0], z_recv.at[back - 1], at(dz=back)).start()
+        remote(2, intra_send.at[1 - core, 0], z_recv.at[chips - 2 + back], at(dz=back, other=True)).start()
+
+    remote(0, intra_send.at[1 - core], sib_recv, at(other=True)).start()
+
     load(HALVES).wait()
-    load(0).wait()
     for k in range(blocks):
         parts = products(k, inter_buf[k, 0], inter_buf[k, 1])
         for j in range(fan_areas):
@@ -152,33 +188,18 @@
                 total = jnp.where(targets[j] == b, rows[j], total)
             x_send[b // SIDE, b % SIDE, t] = total
 
-    def intra(k):
-        for f in range(0, fan, 2):
-            left, right = products(k, intra_buf[k, f], intra_buf[k, f + 1])
-            intra_rows[pl.ds((f * blocks + k) * 8, 8), :] = left
-            intra_rows[pl.ds(((f + 1) * blocks + k) * 8, 8), :] = right
-
-    for k in range(blocks // 2):
-        intra(k)
-
     partners(1, False, send_x)
-    load(1).wait()
-    for k in range(blocks // 2, blocks):
-        intra(k)
-    for t in range(steps):
-        high, low = split(intra_rows[pl.ds(t, half, stride=8), :])
-        grid = jnp.dot(picker, jnp.concatenate([high, low], axis=0), preferred_element_type=F32)
-        for p in range(chips * CORES):
-            intra_send[p % CORES, p // CORES, t] = grid[p * blocks:(p + 1) * blocks, :]
-
-    remote(0, intra_send.at[1 - core], sib_recv, at(other=True)).start()
-
 
     wait(recv_sem, 0, sib_recv)
     for p in range(chips):
         for t in range(steps):
             z_send[p, t] = intra_send[core, p, t] + sib_recv[p, t]
-    partners(0, False, send_z)
+    def send_z_summed(d, peer):
+        @pl.when(jnp.logical_not(jnp.logical_and(is_late, z + d == chips)))
+        def _():
+            send_z(d, peer)
+
+    partners(0, False, send_z_summed)
     entered(1)
     partners(1, True, send_x)
 
@@ -201,8 +222,26 @@
         for i in range(SIDE - 1):
             extra = extra + y_recv[i, t]
         current[t + 1] = current[t + 1] + extra
-    wait(recv_sem, 2, z_recv)
-    for i in range(chips - 1):
+
+    @pl.when(z > 0)
+    def _():
+        wait(recv_sem, 2, z_recv.at[pl.ds(0, chips - 1)])
+
+    @pl.when(z == 0)
+    def _():
+        wait(recv_sem, 2, z_recv)
+        for t in range(steps):
+            extra = z_recv[chips - 1, t]
+            for i in range(chips, chips - 1 + late):
+                extra = extra + z_recv[i, t]
+            z_recv[chips - 1, t] = extra
+
+    @pl.when(z > 0)
+    def _():
+        for t in range(steps):
+            z_recv[chips - 1, t] = jnp.zeros_like(v_ref)
+
+    for i in range(chips):
         current = [current[t] + z_recv[i, t] for t in range(steps)]
 
     potential = v_ref[...]
@@ -213,7 +252,15 @@
 
     wait(send_sem, 0, sib_recv)
     wait(send_sem, 1, x_recv)
-    wait(send_sem, 2, z_recv)
+
+    @pl.when(is_late)
+    def _():
+        wait(send_sem, 2, z_recv.at[pl.ds(0, chips)])
+
+    @pl.when(jnp.logical_not(is_late))
+    def _():
+        wait(send_sem, 2, z_recv.at[pl.ds(0, chips - 1)])
+
     wait(send_sem, 3, y_recv)
 
 
@@ -243,7 +290,7 @@
             pltpu.VMEM((CORES, chips, steps) + tile, F32),
             pltpu.VMEM((chips, steps) + tile, F32),
             pltpu.VMEM((chips, steps) + tile, F32),
-            pltpu.VMEM((chips - 1, steps) + tile, F32),
+            pltpu.VMEM((chips - 1 + chips // 2, steps) + tile, F32),
             pltpu.VMEM((SIDE, SIDE, steps - 1) + tile, F32),
             pltpu.VMEM((SIDE - 1, SIDE, steps - 1) + tile, F32),
             pltpu.VMEM((SIDE, steps - 1) + tile, F32),

time: 15.2 us -> 14.7 us (0.967)
  Pallas kernels: 14.5 us -> 14 us
    pallas_call x1, Pallas kernels: 14.5 us -> 14 us  [body(): pl.pallas_call(kernel, out_shape=[jax.ShapeDtypeStruct(tile, F32)] * 2, i...]
where the time goes in v5:
time: 14.7 us; the launch traced here: 14.6 us
  Pallas kernels  14 us (95%)
  other arithmetic  0.6 us (4%)
    pallas_call x1, Pallas kernels, body(): pl.pallas_call(kernel, out_shape=[jax.ShapeDtypeStruct(tile, F32)] * 2, i...  14 us
    add x1, other arithmetic, body(): return (held + last).reshape(1, blocks * width)  0.6 us

profile of v5, /device:TPU:1, one launch (start us, length us, event | category | flops | bytes accessed | tf_op | source)
XLA Modules:
  0.0 14.6 jit_solution(2449324065883385876)
XLA Ops:
  0.0 14.0 %shard_map.73 = (f32[8,128]{1,0:T(8,128)S(1)}, f32[8,128]{1,0:T(8,128)S(1)}) custom-call(s32[3,8,128]{2,1,0:T(8,128)} %bitcast.14, s32[8,128]{1,0:T(8,128)} %bitcast.15, s32[2,16]{1,0:T(2,128)} %bitcast.18, f32[8,128]{1,0:T(8,128)} %bitcast.16, f32[8,128]{1,0:T(8,128)} %bitcast.17, f32[8,8,128,128]{3,2,1,0:T(8,128)} %bitcast.12, f32[8,2,128,128]{3,2,1,0:T(8,128)} %bitcast.13), custom_call_target="tpu_custom_call" | custom-call | tf_op jit(solution)/shard_map/pallas_call | solution.py:275
  14.0 0.6 %add.3 = f32[8,128]{1,0:T(8,128)} add(f32[8,128]{1,0:T(8,128)S(1)} %get-tuple-element.7, f32[8,128]{1,0:T(8,128)S(1)} %get-tuple-element.8) | non-fusion elementwise | flops 1024 | bytes 12288 | tf_op jit(solution)/shard_map/add | solution.py:319

commit v6 on v5

--- a/solution.py
+++ b/solution.py
@@ -11,7 +11,8 @@
 F32 = jnp.float32
 BF16 = jnp.bfloat16
 SIDE = 4
-HALVES = 2
+PARTS = 4
+INTER_PARTS = 1
 CORES = 2
 
 
@@ -44,6 +45,8 @@
         sec = lax.rem(z + dz, chips) * CORES + (1 - core if other else core)
         return {"area": area, "sec": sec}
 
+    at_corner = x + y == 0
+
     late = chips // 2
     is_late = z >= late
 
@@ -69,10 +72,11 @@
         return pltpu.make_async_copy(src, dst, small_sem.at[i])
 
     def load(k):
-        if k == HALVES:
-            return pltpu.make_async_copy(inter_hbm, inter_buf, load_sem.at[k])
-        half = pl.ds(k * (blocks // HALVES), blocks // HALVES)
-        return pltpu.make_async_copy(intra_hbm.at[half], intra_buf.at[half], load_sem.at[k])
+        src, dst, parts, i = intra_hbm, intra_buf, PARTS, k
+        if k >= PARTS:
+            src, dst, parts, i = inter_hbm, inter_buf, INTER_PARTS, k - PARTS
+        part = pl.ds(i * (blocks // parts), blocks // parts)
+        return pltpu.make_async_copy(src.at[part], dst.at[part], load_sem.at[k])
 
     def remote(i, src, dst, peer):
         return pltpu.make_async_remote_copy(
@@ -99,8 +103,8 @@
         def _():
             pl.semaphore_wait(ready_sem.at[axis], length - 1 - place)
 
-    for k in range(HALVES + 1):
-        load(k).start()
+    for k, priority in ((0, 0), (1, 1), (2, 0), (3, 1), (4, 0)):
+        load(k).start(priority=priority)
     for i in range(3):
         small(i).start()
     barrier = pltpu.get_barrier_semaphore()
@@ -147,17 +151,40 @@
         part = jnp.dot(spikes_of(k), rhs, preferred_element_type=F32)
         return part[:, :width], part[:, width:]
 
+    def inter():
+        for k in range(INTER_PARTS):
+            load(PARTS + k).wait()
+        for k in range(blocks):
+            parts = products(k, inter_buf[k, 0], inter_buf[k, 1])
+            for j in range(fan_areas):
+                inter_rows[j, pl.ds(k * 8, 8), :] = parts[j]
+        for t in range(later):
+            rows = [inter_rows[j, pl.ds(t, blocks, stride=8), :] for j in range(fan_areas)]
+            for b in range(SIDE * SIDE):
+                total = jnp.where(targets[0] == b, rows[0], 0.0)
+                for j in range(1, fan_areas):
+                    total = jnp.where(targets[j] == b, rows[j], total)
+                x_send[b // SIDE, b % SIDE, t] = total
+
+
     def intra(k):
         for f in range(0, fan, 2):
             left, right = products(k, intra_buf[k, f], intra_buf[k, f + 1])
             intra_rows[pl.ds((f * blocks + k) * 8, 8), :] = left
             intra_rows[pl.ds(((f + 1) * blocks + k) * 8, 8), :] = right
 
-    load(0).wait()
+    @pl.when(jnp.logical_not(at_corner))
+    def _():
+        inter()
+        partners(1, False, send_x)
+
+    for k in range(PARTS // 2):
+        load(k).wait()
     for k in range(blocks // 2):
         intra(k)
 
-    load(1).wait()
+    for k in range(PARTS // 2, PARTS):
+        load(k).wait()
     for k in range(blocks // 2, blocks):
         intra(k)
     for t in range(steps):
@@ -175,20 +202,10 @@
 
     remote(0, intra_send.at[1 - core], sib_recv, at(other=True)).start()
 
-    load(HALVES).wait()
-    for k in range(blocks):
-        parts = products(k, inter_buf[k, 0], inter_buf[k, 1])
-        for j in range(fan_areas):
-            inter_rows[j, pl.ds(k * 8, 8), :] = parts[j]
-    for t in range(later):
-        rows = [inter_rows[j, pl.ds(t, blocks, stride=8), :] for j in range(fan_areas)]
-        for b in range(SIDE * SIDE):
-            total = jnp.where(targets[0] == b, rows[0], 0.0)
-            for j in range(1, fan_areas):
-                total = jnp.where(targets[j] == b, rows[j], total)
-            x_send[b // SIDE, b % SIDE, t] = total
-
-    partners(1, False, send_x)
+    @pl.when(at_corner)
+    def _():
+        inter()
+
 
     wait(recv_sem, 0, sib_recv)
     for p in range(chips):
@@ -296,7 +313,7 @@
             pltpu.VMEM((SIDE, steps - 1) + tile, F32),
             pltpu.VMEM((SIDE - 1, steps - 1) + tile, F32),
             pltpu.SemaphoreType.DMA((5,)),
-            pltpu.SemaphoreType.DMA((HALVES + 1,)),
+            pltpu.SemaphoreType.DMA((PARTS + INTER_PARTS,)),
             pltpu.SemaphoreType.DMA((4,)),
             pltpu.SemaphoreType.DMA((4,)),
             pltpu.SemaphoreType.REGULAR((3,)),

time: 14.7 us -> 14.4 us (0.980)
  Pallas kernels: 14 us -> 13.8 us
    pallas_call x1, Pallas kernels: 14 us -> 13.8 us  [body(): pl.pallas_call(kernel, out_shape=[jax.ShapeDtypeStruct(tile, F32)] * 2, i...]
where the time goes in v6:
time: 14.4 us
  Pallas kernels  13.8 us (96%)
  other arithmetic  0.6 us (4%)
    pallas_call x1, Pallas kernels, body(): pl.pallas_call(kernel, out_shape=[jax.ShapeDtypeStruct(tile, F32)] * 2, i...  13.8 us
    add x1, other arithmetic, body(): return (held + last).reshape(1, blocks * width)  0.6 us

profile of v6, /device:TPU:1, one launch (start us, length us, event | category | flops | bytes accessed | tf_op | source)
XLA Modules:
  0.0 14.4 jit_solution(16718334153654952418)
XLA Ops:
  0.0 13.8 %shard_map.73 = (f32[8,128]{1,0:T(8,128)S(1)}, f32[8,128]{1,0:T(8,128)S(1)}) custom-call(s32[3,8,128]{2,1,0:T(8,128)} %bitcast.14, s32[8,128]{1,0:T(8,128)} %bitcast.15, s32[2,16]{1,0:T(2,128)} %bitcast.18, f32[8,128]{1,0:T(8,128)} %bitcast.16, f32[8,128]{1,0:T(8,128)} %bitcast.17, f32[8,8,128,128]{3,2,1,0:T(8,128)} %bitcast.12, f32[8,2,128,128]{3,2,1,0:T(8,128)} %bitcast.13), custom_call_target="tpu_custom_call" | custom-call | tf_op jit(solution)/shard_map/pallas_call | solution.py:292
  13.8 0.6 %add.3 = f32[8,128]{1,0:T(8,128)} add(f32[8,128]{1,0:T(8,128)S(1)} %get-tuple-element.7, f32[8,128]{1,0:T(8,128)S(1)} %get-tuple-element.8) | non-fusion elementwise | flops 1024 | bytes 12288 | tf_op jit(solution)/shard_map/add | solution.py:336

commit v7 on v6

--- a/solution.py
+++ b/solution.py
@@ -103,8 +103,12 @@
         def _():
             pl.semaphore_wait(ready_sem.at[axis], length - 1 - place)
 
-    for k, priority in ((0, 0), (1, 1), (2, 0), (3, 1), (4, 0)):
+    for k, priority in ((0, 0), (1, 1), (2, 0), (3, 1)):
         load(k).start(priority=priority)
+    @pl.when(jnp.logical_not(at_corner))
+    def _():
+        load(PARTS).start()
+
     for i in range(3):
         small(i).start()
     barrier = pltpu.get_barrier_semaphore()
@@ -180,6 +184,11 @@
 
     for k in range(PARTS // 2):
         load(k).wait()
+
+    @pl.when(at_corner)
+    def _():
+        load(PARTS).start()
+
     for k in range(blocks // 2):
         intra(k)
 

time: 14.4 us -> 14.2 us (0.986)
  Pallas kernels: 13.8 us -> 13.5 us
    pallas_call x1, Pallas kernels: 13.8 us -> 13.5 us  [body(): pl.pallas_call(kernel, out_shape=[jax.ShapeDtypeStruct(tile, F32)] * 2, i...]
where the time goes in v7:
time: 14.2 us; the launch traced here: 14.1 us
  Pallas kernels  13.5 us (95%)
  other arithmetic  0.6 us (4%)
    pallas_call x1, Pallas kernels, body(): pl.pallas_call(kernel, out_shape=[jax.ShapeDtypeStruct(tile, F32)] * 2, i...  13.5 us
    add x1, other arithmetic, body(): return (held + last).reshape(1, blocks * width)  0.6 us

profile of v7, /device:TPU:1, one launch (start us, length us, event | category | flops | bytes accessed | tf_op | source)
XLA Modules:
  0.0 14.1 jit_solution(6997185774582197448)
XLA Ops:
  0.0 13.5 %shard_map.73 = (f32[8,128]{1,0:T(8,128)S(1)}, f32[8,128]{1,0:T(8,128)S(1)}) custom-call(s32[3,8,128]{2,1,0:T(8,128)} %bitcast.14, s32[8,128]{1,0:T(8,128)} %bitcast.15, s32[2,16]{1,0:T(2,128)} %bitcast.18, f32[8,128]{1,0:T(8,128)} %bitcast.16, f32[8,128]{1,0:T(8,128)} %bitcast.17, f32[8,8,128,128]{3,2,1,0:T(8,128)} %bitcast.12, f32[8,2,128,128]{3,2,1,0:T(8,128)} %bitcast.13), custom_call_target="tpu_custom_call" | custom-call | tf_op jit(solution)/shard_map/pallas_call | solution.py:301
  13.5 0.6 %add.3 = f32[8,128]{1,0:T(8,128)} add(f32[8,128]{1,0:T(8,128)S(1)} %get-tuple-element.7, f32[8,128]{1,0:T(8,128)S(1)} %get-tuple-element.8) | non-fusion elementwise | flops 1024 | bytes 12288 | tf_op jit(solution)/shard_map/add | solution.py:345
